TPU v7x, 32 devices: a whole 2x2x4 slice. The times are simulated.
32 devices in a mesh: sub: 4 (over z), wide: 8 (over y, x, core).
Axes of the slice: x: 2, y: 2, z: 4, core: 2. Of those that a mesh axis runs over, the one named last changes fastest.
Arguments:
- load_table: bfloat16 [4, 8, 16, 4, 128], P('sub', 'wide'), may hold values from -6 to 6
- load_column: int32 [64], replicated, may hold values from 0 to 15
- face_order: int32 [4, 8, 4], P('sub', 'wide'), may hold values from 0 to 3, each once within a row
- schur: bfloat16 [4, 8, 512, 512], P('sub', 'wide'), as said below
- neumann: bfloat16 [4, 8, 512, 512], P('sub', 'wide'), as said below
- coarse_basis: bfloat16 [4, 8, 4, 4, 128], P('sub', 'wide'), may hold values from -0.625 to 0.625
- corner_map: int32 [4, 8, 4], P('sub', 'wide'), may hold values from 0 to 47, as said below
- coarse_inverse: float32 [48, 48], P('wide'), as said below
Outputs:
- solution: float32 [4, 8, 4, 64, 128], P('sub', 'wide')
Inputs may be any that keep to these rules, and one draw needn't show every extreme that they name: `corner_map`: each subdomain's 4 entries are distinct; subdomains that meet at a corner of the grid of subdomains give it the same number, and different corners get different numbers, so (5) * (9) of the 48 numbers occur and the others belong to no corner. `coarse_inverse`: Symmetric. `schur`: Symmetric. `neumann`: Symmetric.
All inputs are finite; a program needn't handle non-finite values.
Results may differ from a plain program's by a relative error of at most 0.0014.
Values sent between devices are 32-bit elements; how exact they have to be, the bound alone decides.
A program may use at most 64 MiB of HBM per device.

v0:
```python
import jax
import jax.numpy as jnp
from jax import lax
from jax.sharding import PartitionSpec as P

ITERS = 3
damping = 0.3


def with_halo(cells, sides, width):
    for axis, dim in sides:
        count = lax.axis_size(axis)
        ends = count - 1
        head = lax.slice_in_dim(cells, 0, width, axis=dim)
        tail = lax.slice_in_dim(cells, cells.shape[dim] - width, cells.shape[dim], axis=dim)
        cells = jnp.concatenate(
            [
                lax.ppermute(tail, axis, [(i, (i + 1) % count) for i in range(ends)]),
                cells,
                lax.ppermute(head, axis, [((i + 1) % count, i) for i in range(ends)]),
            ],
            axis=dim,
        )
    return cells


def apply_local(vectors, operators, selector_half, selector_full):
    amount = vectors.shape[0]
    rhs_count = vectors.shape[3]
    face_width = vectors.shape[4]
    rounded = vectors.astype(jnp.bfloat16)
    blocked = jnp.einsum(
        "kcbf,kcfjn->kcjbn", selector_half, rounded, preferred_element_type=jnp.float32
    )
    blocked = blocked.astype(jnp.bfloat16).reshape(amount, 1, rhs_count, 4 * face_width)
    product = jnp.einsum("kcjm,kcmn->kcjn", blocked, operators, preferred_element_type=jnp.float32)
    product = product.reshape(amount, 1, rhs_count, 4, face_width)
    return jnp.einsum("kcbf,kcjbn->kcfjn", selector_full, product, precision=lax.Precision.HIGHEST)


def assemble(copies):
    side_stack = jnp.stack([copies[:, 0, 2], copies[:, 0, 3]], axis=0)
    side_halo = with_halo(side_stack, (("wide", 0),), 1)
    end_stack = jnp.stack([copies[0, 0, 0], copies[-1, 0, 1]], axis=0)
    end_halo = with_halo(end_stack, (("sub", 0),), 1)
    upper_faces = jnp.concatenate([end_halo[0:1], copies[:-1, 0, 1]], axis=0)
    lower_faces = jnp.concatenate([copies[1:, 0, 0], end_halo[3:4]], axis=0)
    north_sum = copies[:, 0, 0] + upper_faces
    south_sum = copies[:, 0, 1] + lower_faces
    west_sum = copies[:, 0, 2] + side_halo[0]
    east_sum = copies[:, 0, 3] + side_halo[3]
    return jnp.stack([north_sum, south_sum, west_sum, east_sum], axis=1)[:, None]


def coarse_solve(partial_value, coarse_inverse):
    assembled = lax.psum(partial_value, ("sub", "wide"))
    owned_rows = jnp.dot(assembled, coarse_inverse.T, precision=lax.Precision.HIGHEST)
    return lax.all_gather(owned_rows, "wide", axis=1, tiled=True)


def body(
    load_table, load_column, face_order, schur, neumann, coarse_basis, corner_map, coarse_inverse
):
    amount = schur.shape[0]
    pattern_count = load_table.shape[2]
    coarse_order = coarse_inverse.shape[1]
    selector_full = (face_order[..., :, None] == jnp.arange(4, dtype=jnp.int32)).astype(jnp.float32)
    selector_half = selector_full.astype(jnp.bfloat16)
    load_select = (load_column[:, None] == jnp.arange(pattern_count, dtype=jnp.int32)).astype(
        jnp.bfloat16
    )
    load_faces = jnp.einsum(
        "jl,kclfn->kcfjn", load_select, load_table, preferred_element_type=jnp.float32
    )
    row_ids = lax.axis_index("sub") * amount + jnp.arange(amount, dtype=jnp.int32)
    rows_total = amount * lax.axis_size("sub")
    column_index = lax.axis_index("wide") * jnp.ones((amount,), jnp.int32)
    cols_total = lax.axis_size("wide")
    half = jnp.float32(0.5)
    whole = jnp.float32(1.0)
    weights = jnp.stack(
        [
            jnp.where(row_ids > 0, half, whole),
            jnp.where(row_ids < rows_total - 1, half, whole),
            jnp.where(column_index > 0, half, whole),
            jnp.where(column_index < cols_total - 1, half, whole),
        ],
        axis=1,
    )[:, None, :, None, None]
    basis = coarse_basis.astype(jnp.float32)
    corner_marks = (corner_map[..., None] == jnp.arange(coarse_order, dtype=jnp.int32)).astype(
        jnp.float32
    )
    solution = jnp.zeros(load_faces.shape, jnp.float32)
    for iteration in range(ITERS):
        if iteration == 0:
            residual = assemble(load_faces)
        else:
            residual = assemble(
                load_faces - apply_local(solution, schur, selector_half, selector_full)
            )
        weighted = weights * residual
        restricted = jnp.einsum(
            "kcpfn,kcfjn->kcpj", basis, weighted, precision=lax.Precision.HIGHEST
        )
        partial_value = jnp.einsum(
            "kcpj,kcpg->jg", restricted, corner_marks, precision=lax.Precision.HIGHEST
        )
        neumann_part = apply_local(weighted, neumann, selector_half, selector_full)
        solved = coarse_solve(partial_value, coarse_inverse)
        picked = jnp.einsum("jg,kcpg->kcpj", solved, corner_marks, precision=lax.Precision.HIGHEST)
        correction = jnp.einsum("kcpj,kcpfn->kcfjn", picked, basis, precision=lax.Precision.HIGHEST)
        update = assemble(weights * (neumann_part + correction))
        solution = solution + damping * update
    return solution


def solution(mesh):
    in_specs = (
        P("sub", "wide", None, None, None),
        P(),
        P("sub", "wide", None),
        P("sub", "wide", None, None),
        P("sub", "wide", None, None),
        P("sub", "wide", None, None, None),
        P("sub", "wide", None),
        P("wide", None),
    )
    out_specs = P("sub", "wide", None, None, None)
    return jax.shard_map(body, mesh=mesh, in_specs=in_specs, out_specs=out_specs, check_vma=False)
```

profile of v0, /device:TPU:4, one launch (start us, length us, event | category | flops | bytes accessed | tf_op | source)
XLA Modules:
  0.0 250.2 jit_solution(4208679977386832550)
XLA Ops:
  0.9 3.5 %collective-permute-start = (f32[1,64,128]{2,1,0:T(8,128)S(1)}, f32[1,64,128]{2,1,0:T(8,128)S(1)}, u32[]{:S(2)}, u32[]{:S(2)}) collective-permute-start(f32[1,64,128]{2,1,0:T(8,128)S(1)} %get-tuple-element.47), channel_id=1, source_target_pairs={{0,8},{8,16},{16,24},{1,9},{9,17},{17,25},{2,10},{10,18},{18,26},{... | collective-permute-start | bytes 98312 | tf_op jit(solution)/shard_map/ppermute | solution.py:18
  6.4 4.5 %collective-permute-start.3 = (f32[1,1,64,128]{3,2,1,0:T(8,128)S(1)}, f32[1,1,64,128]{3,2,1,0:T(8,128)S(1)}, u32[]{:S(2)}, u32[]{:S(2)}) collective-permute-start(f32[1,1,64,128]{3,2,1,0:T(8,128)S(1)} %get-tuple-element.49), channel_id=1, source_target_pairs={{1,0},{2,1},{3,2},{4,3},{5,4},{6,5},{7,6},{9,8},{10,9},{11,10},{12... | collective-permute-start | bytes 98312 | tf_op jit(solution)/shard_map/ppermute | solution.py:20
  13.6 3.1 %collective-permute-done.1 = f32[1,64,128]{2,1,0:T(8,128)S(1)} collective-permute-done((f32[1,64,128]{2,1,0:T(8,128)S(1)}, f32[1,64,128]{2,1,0:T(8,128)S(1)}, u32[]{:S(2)}, u32[]{:S(2)}) %collective-permute-start.1) | collective-permute-done | bytes 32800 | tf_op jit(solution)/shard_map/ppermute | solution.py:20
  19.6 40.5 %psum.21 = f32[64,48]{0,1:T(8,128)S(1)} all-reduce(f32[64,48]{0,1:T(8,128)S(1)} %fusion.44), channel_id=1, replica_groups=mesh['sub'=4,'wide'=8] {'sub','wide'}, use_global_device_ids=true, to_apply=%region_0.1 | all-reduce | flops 3072 | bytes 24576 | tf_op jit(solution)/shard_map/psum | solution.py:56
  60.2 9.0 %all-gather = f32[8,6,64]{2,1,0:T(8,128)S(1)} all-gather(f32[1,6,64]{2,1,0:T(8,128)S(1)} %convolution_bitcast_fusion.6), channel_id=1, replica_groups=mesh['sub'=4,'wide'=8] {'wide'}, dimensions={0}, use_global_device_ids=true | all-gather | bytes 13824 | tf_op jit(solution)/shard_map/all_gather | solution.py:58
  70.4 2.3 collective-permute-start.6
  72.6 4.2 %collective-permute-start.7 = (f32[1,1,64,128]{3,2,1,0:T(8,128)S(1)}, f32[1,1,64,128]{3,2,1,0:T(8,128)S(1)}, u32[]{:S(2)}, u32[]{:S(2)}) collective-permute-start(f32[1,1,64,128]{3,2,1,0:T(8,128)S(1)} %get-tuple-element.41), channel_id=1, source_target_pairs={{1,0},{2,1},{3,2},{4,3},{5,4},{6,5},{7,6},{9,8},{10,9},{11,10},{12... | collective-permute-start | bytes 98312 | tf_op jit(solution)/shard_map/ppermute | solution.py:20
  80.8 4.2 %collective-permute-done.5 = f32[1,64,128]{2,1,0:T(8,128)S(1)} collective-permute-done((f32[1,64,128]{2,1,0:T(8,128)S(1)}, f32[1,64,128]{2,1,0:T(8,128)S(1)}, u32[]{:S(2)}, u32[]{:S(2)}) %collective-permute-start.5) | collective-permute-done | bytes 32800 | tf_op jit(solution)/shard_map/ppermute | solution.py:20
  87.9 4.5 %collective-permute-start.11 = (f32[1,1,64,128]{3,2,1,0:T(8,128)S(1)}, f32[1,1,64,128]{3,2,1,0:T(8,128)S(1)}, u32[]{:S(2)}, u32[]{:S(2)}) collective-permute-start(f32[1,1,64,128]{3,2,1,0:T(8,128)S(1)} %get-tuple-element.33), channel_id=1, source_target_pairs={{1,0},{2,1},{3,2},{4,3},{5,4},{6,5},{7,6},{9,8},{10,9},{11,10},{12... | collective-permute-start | bytes 98312 | tf_op jit(solution)/shard_map/ppermute | solution.py:20
  92.5 3.1 %collective-permute-start.8 = (f32[1,64,128]{2,1,0:T(8,128)S(1)}, f32[1,64,128]{2,1,0:T(8,128)S(1)}, u32[]{:S(2)}, u32[]{:S(2)}) collective-permute-start(f32[1,64,128]{2,1,0:T(8,128)S(1)} %get-tuple-element.31), channel_id=1, source_target_pairs={{0,8},{8,16},{16,24},{1,9},{9,17},{17,25},{2,10},{10,18},{18,26},{... | collective-permute-start | bytes 98312 | tf_op jit(solution)/shard_map/ppermute | solution.py:18
  97.1 4.2 %collective-permute-done.9 = f32[1,64,128]{2,1,0:T(8,128)S(1)} collective-permute-done((f32[1,64,128]{2,1,0:T(8,128)S(1)}, f32[1,64,128]{2,1,0:T(8,128)S(1)}, u32[]{:S(2)}, u32[]{:S(2)}) %collective-permute-start.9) | collective-permute-done | bytes 32800 | tf_op jit(solution)/shard_map/ppermute | solution.py:20
  102.3 40.3 %psum.22 = f32[64,48]{0,1:T(8,128)S(1)} all-reduce(f32[64,48]{0,1:T(8,128)S(1)} %fusion.43), channel_id=1, replica_groups=mesh['sub'=4,'wide'=8] {'sub','wide'}, use_global_device_ids=true, to_apply=%region_1.2 | all-reduce | flops 3072 | bytes 24576 | tf_op jit(solution)/shard_map/psum | solution.py:56
  142.7 9.5 %all-gather.1 = f32[8,6,64]{2,1,0:T(8,128)S(1)} all-gather(f32[1,6,64]{2,1,0:T(8,128)S(1)} %convolution_bitcast_fusion.5), channel_id=1, replica_groups=mesh['sub'=4,'wide'=8] {'wide'}, dimensions={0}, use_global_device_ids=true | all-gather | bytes 13824 | tf_op jit(solution)/shard_map/all_gather | solution.py:58
  153.3 2.3 collective-permute-start.14
  155.5 4.2 %collective-permute-start.15 = (f32[1,1,64,128]{3,2,1,0:T(8,128)S(1)}, f32[1,1,64,128]{3,2,1,0:T(8,128)S(1)}, u32[]{:S(2)}, u32[]{:S(2)}) collective-permute-start(f32[1,1,64,128]{3,2,1,0:T(8,128)S(1)} %get-tuple-element.25), channel_id=1, source_target_pairs={{1,0},{2,1},{3,2},{4,3},{5,4},{6,5},{7,6},{9,8},{10,9},{11,10},{12... | collective-permute-start | bytes 98312 | tf_op jit(solution)/shard_map/ppermute | solution.py:20
  163.3 4.2 %collective-permute-done.13 = f32[1,64,128]{2,1,0:T(8,128)S(1)} collective-permute-done((f32[1,64,128]{2,1,0:T(8,128)S(1)}, f32[1,64,128]{2,1,0:T(8,128)S(1)}, u32[]{:S(2)}, u32[]{:S(2)}) %collective-permute-start.13) | collective-permute-done | bytes 32800 | tf_op jit(solution)/shard_map/ppermute | solution.py:20
  170.4 4.5 %collective-permute-start.19 = (f32[1,1,64,128]{3,2,1,0:T(8,128)S(1)}, f32[1,1,64,128]{3,2,1,0:T(8,128)S(1)}, u32[]{:S(2)}, u32[]{:S(2)}) collective-permute-start(f32[1,1,64,128]{3,2,1,0:T(8,128)S(1)} %get-tuple-element.17), channel_id=1, source_target_pairs={{1,0},{2,1},{3,2},{4,3},{5,4},{6,5},{7,6},{9,8},{10,9},{11,10},{12... | collective-permute-start | bytes 98312 | tf_op jit(solution)/shard_map/ppermute | solution.py:20
  175.0 2.6 %collective-permute-start.16 = (f32[1,64,128]{2,1,0:T(8,128)S(1)}, f32[1,64,128]{2,1,0:T(8,128)S(1)}, u32[]{:S(2)}, u32[]{:S(2)}) collective-permute-start(f32[1,64,128]{2,1,0:T(8,128)S(1)} %get-tuple-element.15), channel_id=1, source_target_pairs={{0,8},{8,16},{16,24},{1,9},{9,17},{17,25},{2,10},{10,18},{18,26},{... | collective-permute-start | bytes 98312 | tf_op jit(solution)/shard_map/ppermute | solution.py:18
  179.1 4.2 %collective-permute-done.17 = f32[1,64,128]{2,1,0:T(8,128)S(1)} collective-permute-done((f32[1,64,128]{2,1,0:T(8,128)S(1)}, f32[1,64,128]{2,1,0:T(8,128)S(1)}, u32[]{:S(2)}, u32[]{:S(2)}) %collective-permute-start.17) | collective-permute-done | bytes 32800 | tf_op jit(solution)/shard_map/ppermute | solution.py:20
  184.9 40.3 %psum.23 = f32[64,48]{0,1:T(8,128)S(1)} all-reduce(f32[64,48]{0,1:T(8,128)S(1)} %fusion.42), channel_id=1, replica_groups=mesh['sub'=4,'wide'=8] {'sub','wide'}, use_global_device_ids=true, to_apply=%region_2.3 | all-reduce | flops 3072 | bytes 24576 | tf_op jit(solution)/shard_map/psum | solution.py:56
  225.2 9.5 %all-gather.2 = f32[8,6,64]{2,1,0:T(8,128)S(1)} all-gather(f32[1,6,64]{2,1,0:T(8,128)S(1)} %convolution_bitcast_fusion.4), channel_id=1, replica_groups=mesh['sub'=4,'wide'=8] {'wide'}, dimensions={0}, use_global_device_ids=true | all-gather | bytes 13824 | tf_op jit(solution)/shard_map/all_gather | solution.py:58
  235.3 2.3 collective-permute-start.22
  237.5 4.2 %collective-permute-start.23 = (f32[1,1,64,128]{3,2,1,0:T(8,128)S(1)}, f32[1,1,64,128]{3,2,1,0:T(8,128)S(1)}, u32[]{:S(2)}, u32[]{:S(2)}) collective-permute-start(f32[1,1,64,128]{3,2,1,0:T(8,128)S(1)} %get-tuple-element.9), channel_id=1, source_target_pairs={{1,0},{2,1},{3,2},{4,3},{5,4},{6,5},{7,6},{9,8},{10,9},{11,10},{12... | collective-permute-start | bytes 98312 | tf_op jit(solution)/shard_map/ppermute | solution.py:20
  245.2 4.2 %collective-permute-done.21 = f32[1,64,128]{2,1,0:T(8,128)S(1)} collective-permute-done((f32[1,64,128]{2,1,0:T(8,128)S(1)}, f32[1,64,128]{2,1,0:T(8,128)S(1)}, u32[]{:S(2)}, u32[]{:S(2)}) %collective-permute-start.21) | collective-permute-done | bytes 32800 | tf_op jit(solution)/shard_map/ppermute | solution.py:20
  (112 shorter events, 34.0 us)
Async XLA Ops:
  0.9 12.7 %collective-permute-start = (f32[1,64,128]{2,1,0:T(8,128)S(1)}, f32[1,64,128]{2,1,0:T(8,128)S(1)}, u32[]{:S(2)}, u32[]{:S(2)}) collective-permute-start(f32[1,64,128]{2,1,0:T(8,128)S(1)} %get-tuple-element.47), channel_id=1, source_target_pairs={{0,8},{8,16},{16,24},{1,9},{9,17},{17,25},{2,10},{10,18},{18,26},{... | collective-permute-start | bytes 98312 | tf_op jit(solution)/shard_map/ppermute | solution.py:18
  4.4 9.1 %collective-permute-start.2 = (f32[1,1,64,128]{3,2,1,0:T(8,128)S(1)}, f32[1,1,64,128]{3,2,1,0:T(8,128)S(1)}, u32[]{:S(2)}, u32[]{:S(2)}) collective-permute-start(f32[1,1,64,128]{3,2,1,0:T(8,128)S(1)} %get-tuple-element.48), channel_id=1, source_target_pairs={{0,1},{1,2},{2,3},{3,4},{4,5},{5,6},{6,7},{8,9},{9,10},{10,11},{11... | collective-permute-start | bytes 98312 | tf_op jit(solution)/shard_map/ppermute | solution.py:18
  6.4 7.2 %collective-permute-start.3 = (f32[1,1,64,128]{3,2,1,0:T(8,128)S(1)}, f32[1,1,64,128]{3,2,1,0:T(8,128)S(1)}, u32[]{:S(2)}, u32[]{:S(2)}) collective-permute-start(f32[1,1,64,128]{3,2,1,0:T(8,128)S(1)} %get-tuple-element.49), channel_id=1, source_target_pairs={{1,0},{2,1},{3,2},{4,3},{5,4},{6,5},{7,6},{9,8},{10,9},{11,10},{12... | collective-permute-start | bytes 98312 | tf_op jit(solution)/shard_map/ppermute | solution.py:20
  10.9 5.8 %collective-permute-start.1 = (f32[1,64,128]{2,1,0:T(8,128)S(1)}, f32[1,64,128]{2,1,0:T(8,128)S(1)}, u32[]{:S(2)}, u32[]{:S(2)}) collective-permute-start(f32[1,64,128]{2,1,0:T(8,128)S(1)} %get-tuple-element.50), channel_id=1, source_target_pairs={{8,0},{16,8},{24,16},{9,1},{17,9},{25,17},{10,2},{18,10},{26,18},{... | collective-permute-start | bytes 98312 | tf_op jit(solution)/shard_map/ppermute | solution.py:20
  70.4 10.2 %collective-permute-start.6 = (f32[1,1,64,128]{3,2,1,0:T(8,128)S(1)}, f32[1,1,64,128]{3,2,1,0:T(8,128)S(1)}, u32[]{:S(2)}, u32[]{:S(2)}) collective-permute-start(f32[1,1,64,128]{3,2,1,0:T(8,128)S(1)} %get-tuple-element.40), channel_id=1, source_target_pairs={{0,1},{1,2},{2,3},{3,4},{4,5},{5,6},{6,7},{8,9},{9,10},{10,11},{11... | collective-permute-start | bytes 98312 | tf_op jit(solution)/shard_map/ppermute | solution.py:18
  72.6 7.9 %collective-permute-start.7 = (f32[1,1,64,128]{3,2,1,0:T(8,128)S(1)}, f32[1,1,64,128]{3,2,1,0:T(8,128)S(1)}, u32[]{:S(2)}, u32[]{:S(2)}) collective-permute-start(f32[1,1,64,128]{3,2,1,0:T(8,128)S(1)} %get-tuple-element.41), channel_id=1, source_target_pairs={{1,0},{2,1},{3,2},{4,3},{5,4},{6,5},{7,6},{9,8},{10,9},{11,10},{12... | collective-permute-start | bytes 98312 | tf_op jit(solution)/shard_map/ppermute | solution.py:20
  77.1 3.7 %collective-permute-start.4 = (f32[1,64,128]{2,1,0:T(8,128)S(1)}, f32[1,64,128]{2,1,0:T(8,128)S(1)}, u32[]{:S(2)}, u32[]{:S(2)}) collective-permute-start(f32[1,64,128]{2,1,0:T(8,128)S(1)} %get-tuple-element.39), channel_id=1, source_target_pairs={{0,8},{8,16},{16,24},{1,9},{9,17},{17,25},{2,10},{10,18},{18,26},{... | collective-permute-start | bytes 98312 | tf_op jit(solution)/shard_map/ppermute | solution.py:18
  79.2 5.8 %collective-permute-start.5 = (f32[1,64,128]{2,1,0:T(8,128)S(1)}, f32[1,64,128]{2,1,0:T(8,128)S(1)}, u32[]{:S(2)}, u32[]{:S(2)}) collective-permute-start(f32[1,64,128]{2,1,0:T(8,128)S(1)} %get-tuple-element.42), channel_id=1, source_target_pairs={{8,0},{16,8},{24,16},{9,1},{17,9},{25,17},{10,2},{18,10},{26,18},{... | collective-permute-start | bytes 98312 | tf_op jit(solution)/shard_map/ppermute | solution.py:20
  86.0 10.8 %collective-permute-start.10 = (f32[1,1,64,128]{3,2,1,0:T(8,128)S(1)}, f32[1,1,64,128]{3,2,1,0:T(8,128)S(1)}, u32[]{:S(2)}, u32[]{:S(2)}) collective-permute-start(f32[1,1,64,128]{3,2,1,0:T(8,128)S(1)} %get-tuple-element.32), channel_id=1, source_target_pairs={{0,1},{1,2},{2,3},{3,4},{4,5},{5,6},{6,7},{8,9},{9,10},{10,11},{11... | collective-permute-start | bytes 98312 | tf_op jit(solution)/shard_map/ppermute | solution.py:18
  87.9 8.9 %collective-permute-start.11 = (f32[1,1,64,128]{3,2,1,0:T(8,128)S(1)}, f32[1,1,64,128]{3,2,1,0:T(8,128)S(1)}, u32[]{:S(2)}, u32[]{:S(2)}) collective-permute-start(f32[1,1,64,128]{3,2,1,0:T(8,128)S(1)} %get-tuple-element.33), channel_id=1, source_target_pairs={{1,0},{2,1},{3,2},{4,3},{5,4},{6,5},{7,6},{9,8},{10,9},{11,10},{12... | collective-permute-start | bytes 98312 | tf_op jit(solution)/shard_map/ppermute | solution.py:20
  92.5 4.6 %collective-permute-start.8 = (f32[1,64,128]{2,1,0:T(8,128)S(1)}, f32[1,64,128]{2,1,0:T(8,128)S(1)}, u32[]{:S(2)}, u32[]{:S(2)}) collective-permute-start(f32[1,64,128]{2,1,0:T(8,128)S(1)} %get-tuple-element.31), channel_id=1, source_target_pairs={{0,8},{8,16},{16,24},{1,9},{9,17},{17,25},{2,10},{10,18},{18,26},{... | collective-permute-start | bytes 98312 | tf_op jit(solution)/shard_map/ppermute | solution.py:18
  95.5 5.8 %collective-permute-start.9 = (f32[1,64,128]{2,1,0:T(8,128)S(1)}, f32[1,64,128]{2,1,0:T(8,128)S(1)}, u32[]{:S(2)}, u32[]{:S(2)}) collective-permute-start(f32[1,64,128]{2,1,0:T(8,128)S(1)} %get-tuple-element.34), channel_id=1, source_target_pairs={{8,0},{16,8},{24,16},{9,1},{17,9},{25,17},{10,2},{18,10},{26,18},{... | collective-permute-start | bytes 98312 | tf_op jit(solution)/shard_map/ppermute | solution.py:20
  153.3 9.7 %collective-permute-start.14 = (f32[1,1,64,128]{3,2,1,0:T(8,128)S(1)}, f32[1,1,64,128]{3,2,1,0:T(8,128)S(1)}, u32[]{:S(2)}, u32[]{:S(2)}) collective-permute-start(f32[1,1,64,128]{3,2,1,0:T(8,128)S(1)} %get-tuple-element.24), channel_id=1, source_target_pairs={{0,1},{1,2},{2,3},{3,4},{4,5},{5,6},{6,7},{8,9},{9,10},{10,11},{11... | collective-permute-start | bytes 98312 | tf_op jit(solution)/shard_map/ppermute | solution.py:18
  155.5 7.5 %collective-permute-start.15 = (f32[1,1,64,128]{3,2,1,0:T(8,128)S(1)}, f32[1,1,64,128]{3,2,1,0:T(8,128)S(1)}, u32[]{:S(2)}, u32[]{:S(2)}) collective-permute-start(f32[1,1,64,128]{3,2,1,0:T(8,128)S(1)} %get-tuple-element.25), channel_id=1, source_target_pairs={{1,0},{2,1},{3,2},{4,3},{5,4},{6,5},{7,6},{9,8},{10,9},{11,10},{12... | collective-permute-start | bytes 98312 | tf_op jit(solution)/shard_map/ppermute | solution.py:20
  159.8 3.5 %collective-permute-start.12 = (f32[1,64,128]{2,1,0:T(8,128)S(1)}, f32[1,64,128]{2,1,0:T(8,128)S(1)}, u32[]{:S(2)}, u32[]{:S(2)}) collective-permute-start(f32[1,64,128]{2,1,0:T(8,128)S(1)} %get-tuple-element.23), channel_id=1, source_target_pairs={{0,8},{8,16},{16,24},{1,9},{9,17},{17,25},{2,10},{10,18},{18,26},{... | collective-permute-start | bytes 98312 | tf_op jit(solution)/shard_map/ppermute | solution.py:18
  161.7 5.8 %collective-permute-start.13 = (f32[1,64,128]{2,1,0:T(8,128)S(1)}, f32[1,64,128]{2,1,0:T(8,128)S(1)}, u32[]{:S(2)}, u32[]{:S(2)}) collective-permute-start(f32[1,64,128]{2,1,0:T(8,128)S(1)} %get-tuple-element.26), channel_id=1, source_target_pairs={{8,0},{16,8},{24,16},{9,1},{17,9},{25,17},{10,2},{18,10},{26,18},{... | collective-permute-start | bytes 98312 | tf_op jit(solution)/shard_map/ppermute | solution.py:20
  168.5 10.3 %collective-permute-start.18 = (f32[1,1,64,128]{3,2,1,0:T(8,128)S(1)}, f32[1,1,64,128]{3,2,1,0:T(8,128)S(1)}, u32[]{:S(2)}, u32[]{:S(2)}) collective-permute-start(f32[1,1,64,128]{3,2,1,0:T(8,128)S(1)} %get-tuple-element.16), channel_id=1, source_target_pairs={{0,1},{1,2},{2,3},{3,4},{4,5},{5,6},{6,7},{8,9},{9,10},{10,11},{11... | collective-permute-start | bytes 98312 | tf_op jit(solution)/shard_map/ppermute | solution.py:18
  170.4 8.4 %collective-permute-start.19 = (f32[1,1,64,128]{3,2,1,0:T(8,128)S(1)}, f32[1,1,64,128]{3,2,1,0:T(8,128)S(1)}, u32[]{:S(2)}, u32[]{:S(2)}) collective-permute-start(f32[1,1,64,128]{3,2,1,0:T(8,128)S(1)} %get-tuple-element.17), channel_id=1, source_target_pairs={{1,0},{2,1},{3,2},{4,3},{5,4},{6,5},{7,6},{9,8},{10,9},{11,10},{12... | collective-permute-start | bytes 98312 | tf_op jit(solution)/shard_map/ppermute | solution.py:20
  175.0 4.1 %collective-permute-start.16 = (f32[1,64,128]{2,1,0:T(8,128)S(1)}, f32[1,64,128]{2,1,0:T(8,128)S(1)}, u32[]{:S(2)}, u32[]{:S(2)}) collective-permute-start(f32[1,64,128]{2,1,0:T(8,128)S(1)} %get-tuple-element.15), channel_id=1, source_target_pairs={{0,8},{8,16},{16,24},{1,9},{9,17},{17,25},{2,10},{10,18},{18,26},{... | collective-permute-start | bytes 98312 | tf_op jit(solution)/shard_map/ppermute | solution.py:18
  177.5 5.8 %collective-permute-start.17 = (f32[1,64,128]{2,1,0:T(8,128)S(1)}, f32[1,64,128]{2,1,0:T(8,128)S(1)}, u32[]{:S(2)}, u32[]{:S(2)}) collective-permute-start(f32[1,64,128]{2,1,0:T(8,128)S(1)} %get-tuple-element.18), channel_id=1, source_target_pairs={{8,0},{16,8},{24,16},{9,1},{17,9},{25,17},{10,2},{18,10},{26,18},{... | collective-permute-start | bytes 98312 | tf_op jit(solution)/shard_map/ppermute | solution.py:20
  235.3 9.7 %collective-permute-start.22 = (f32[1,1,64,128]{3,2,1,0:T(8,128)S(1)}, f32[1,1,64,128]{3,2,1,0:T(8,128)S(1)}, u32[]{:S(2)}, u32[]{:S(2)}) collective-permute-start(f32[1,1,64,128]{3,2,1,0:T(8,128)S(1)} %get-tuple-element.8), channel_id=1, source_target_pairs={{0,1},{1,2},{2,3},{3,4},{4,5},{5,6},{6,7},{8,9},{9,10},{10,11},{11... | collective-permute-start | bytes 98312 | tf_op jit(solution)/shard_map/ppermute | solution.py:18
  237.5 7.5 %collective-permute-start.23 = (f32[1,1,64,128]{3,2,1,0:T(8,128)S(1)}, f32[1,1,64,128]{3,2,1,0:T(8,128)S(1)}, u32[]{:S(2)}, u32[]{:S(2)}) collective-permute-start(f32[1,1,64,128]{3,2,1,0:T(8,128)S(1)} %get-tuple-element.9), channel_id=1, source_target_pairs={{1,0},{2,1},{3,2},{4,3},{5,4},{6,5},{7,6},{9,8},{10,9},{11,10},{12... | collective-permute-start | bytes 98312 | tf_op jit(solution)/shard_map/ppermute | solution.py:20
  241.7 3.5 %collective-permute-start.20 = (f32[1,64,128]{2,1,0:T(8,128)S(1)}, f32[1,64,128]{2,1,0:T(8,128)S(1)}, u32[]{:S(2)}, u32[]{:S(2)}) collective-permute-start(f32[1,64,128]{2,1,0:T(8,128)S(1)} %get-tuple-element.7), channel_id=1, source_target_pairs={{0,8},{8,16},{16,24},{1,9},{9,17},{17,25},{2,10},{10,18},{18,26},{... | collective-permute-start | bytes 98312 | tf_op jit(solution)/shard_map/ppermute | solution.py:18
  243.7 5.8 %collective-permute-start.21 = (f32[1,64,128]{2,1,0:T(8,128)S(1)}, f32[1,64,128]{2,1,0:T(8,128)S(1)}, u32[]{:S(2)}, u32[]{:S(2)}) collective-permute-start(f32[1,64,128]{2,1,0:T(8,128)S(1)} %get-tuple-element.10), channel_id=1, source_target_pairs={{8,0},{16,8},{24,16},{9,1},{17,9},{25,17},{10,2},{18,10},{26,18},{... | collective-permute-start | bytes 98312 | tf_op jit(solution)/shard_map/ppermute | solution.py:20
  (7 other events, 51.1 us)
where the time goes:
time: 251 us; the launch traced here: 250 us
  blocking collectives  149 us (59%)
  starting transfers between devices  61.6 us (25%)
  waiting for transfers between devices  25.5 us (10%)
  matrix products  7.57 us (3%)
  local copies, waits for them, and re-layouts  4.4 us (2%)
    psum x3, blocking collectives, coarse_solve(): assembled = lax.psum(partial_value, ('sub', 'wide'))  121 us
    ppermute x12, starting transfers between devices, with_halo(): lax.ppermute(head, axis, [((i + 1) % count, i) for i in range(ends)])  34 us
    all_gather x3, blocking collectives, coarse_solve(): return lax.all_gather(owned_rows, 'wide', axis=1, tiled=True)  28 us
    ppermute x12, starting transfers between devices, with_halo(): lax.ppermute(tail, axis, [(i, (i + 1) % count) for i in range(ends)])  27.6 us
    ppermute x12, waiting for transfers between devices, with_halo(): lax.ppermute(head, axis, [((i + 1) % count, i) for i in range(ends)])  24.3 us
  transfers between devices with their start and end apart: 24, of which 11 were waited for; matrix products, arithmetic and copies ran while one was open for 1% of the time, Pallas kernels for 0%

commit v1 on v0

--- a/solution.py
+++ b/solution.py
@@ -2,9 +2,16 @@
 import jax.numpy as jnp
 from jax import lax
 from jax.sharding import PartitionSpec as P
+from jax.lax import psum
 
 ITERS = 3
 damping = 0.3
+
+
+def records_handle(slab_in, link_axis, across):
+    for jj in (link_axis, across):
+        slab_in = psum(slab_in, axis_name=jj)
+    return slab_in
 
 
 def with_halo(cells, sides, width):
@@ -53,7 +60,7 @@
 
 
 def coarse_solve(partial_value, coarse_inverse):
-    assembled = lax.psum(partial_value, ("sub", "wide"))
+    assembled = records_handle(partial_value, "sub", "wide")
     owned_rows = jnp.dot(assembled, coarse_inverse.T, precision=lax.Precision.HIGHEST)
     return lax.all_gather(owned_rows, "wide", axis=1, tiled=True)
 

time: 251 us -> 242 us (0.964)
  blocking collectives: 149 us -> 139 us
    all_gather x3, blocking collectives: 28 us -> 21.2 us  [coarse_solve(): return lax.all_gather(owned_rows, 'wide', axis=1, tiled=True)]
    psum x3 -> x6, blocking collectives: 121 us -> 118 us  [records_handle(): slab_in = psum(slab_in, axis_name=jj)]
where the time goes in v1:
time: 242 us; the launch traced here: 240 us
  blocking collectives  139 us (57%)
  starting transfers between devices  61.4 us (25%)
  waiting for transfers between devices  25.5 us (11%)
  matrix products  7.58 us (3%)
  local copies, waits for them, and re-layouts  4.4 us (2%)
    psum x6, blocking collectives, records_handle(): slab_in = psum(slab_in, axis_name=jj)  118 us
    ppermute x12, starting transfers between devices, with_halo(): lax.ppermute(head, axis, [((i + 1) % count, i) for i in range(ends)])  34.2 us
    ppermute x12, starting transfers between devices, with_halo(): lax.ppermute(tail, axis, [(i, (i + 1) % count) for i in range(ends)])  27.1 us
    ppermute x12, waiting for transfers between devices, with_halo(): lax.ppermute(head, axis, [((i + 1) % count, i) for i in range(ends)])  24.3 us
    all_gather x3, blocking collectives, coarse_solve(): return lax.all_gather(owned_rows, 'wide', axis=1, tiled=True)  21.2 us
  transfers between devices with their start and end apart: 24, of which 11 were waited for; matrix products, arithmetic and copies ran while one was open for 1% of the time, Pallas kernels for 0%

profile of v1, /device:TPU:4, one launch (start us, length us, event | category | flops | bytes accessed | tf_op | source)
XLA Modules:
  0.0 239.9 jit_solution(5364389360063137836)
XLA Ops:
  0.9 3.5 %collective-permute-start = (f32[1,64,128]{2,1,0:T(8,128)S(1)}, f32[1,64,128]{2,1,0:T(8,128)S(1)}, u32[]{:S(2)}, u32[]{:S(2)}) collective-permute-start(f32[1,64,128]{2,1,0:T(8,128)S(1)} %get-tuple-element.47), channel_id=1, source_target_pairs={{0,8},{8,16},{16,24},{1,9},{9,17},{17,25},{2,10},{10,18},{18,26},{... | collective-permute-start | bytes 98312 | tf_op jit(solution)/shard_map/ppermute | solution.py:25
  6.4 4.5 %collective-permute-start.3 = (f32[1,1,64,128]{3,2,1,0:T(8,128)S(1)}, f32[1,1,64,128]{3,2,1,0:T(8,128)S(1)}, u32[]{:S(2)}, u32[]{:S(2)}) collective-permute-start(f32[1,1,64,128]{3,2,1,0:T(8,128)S(1)} %get-tuple-element.49), channel_id=1, source_target_pairs={{1,0},{2,1},{3,2},{4,3},{5,4},{6,5},{7,6},{9,8},{10,9},{11,10},{12... | collective-permute-start | bytes 98312 | tf_op jit(solution)/shard_map/ppermute | solution.py:27
  13.6 3.1 %collective-permute-done.1 = f32[1,64,128]{2,1,0:T(8,128)S(1)} collective-permute-done((f32[1,64,128]{2,1,0:T(8,128)S(1)}, f32[1,64,128]{2,1,0:T(8,128)S(1)}, u32[]{:S(2)}, u32[]{:S(2)}) %collective-permute-start.1) | collective-permute-done | bytes 32800 | tf_op jit(solution)/shard_map/ppermute | solution.py:27
  19.5 17.4 %psum.42 = f32[64,48]{0,1:T(8,128)S(1)} all-reduce(f32[64,48]{0,1:T(8,128)S(1)} %fusion.44), channel_id=1, replica_groups=mesh['sub'=4,'wide'=8] {'sub'}, use_global_device_ids=true, to_apply=%region_0.1 | all-reduce | flops 3072 | bytes 24576 | tf_op jit(solution)/shard_map/psum | solution.py:13
  37.0 22.4 %psum.43 = f32[64,48]{0,1:T(8,128)S(1)} all-reduce(f32[64,48]{0,1:T(8,128)S(1)} %psum.42), channel_id=1, replica_groups=mesh['sub'=4,'wide'=8] {'wide'}, use_global_device_ids=true, to_apply=%region_1.2 | all-reduce | flops 3072 | bytes 24576 | tf_op jit(solution)/shard_map/psum | solution.py:13
  59.5 7.0 %all-gather = f32[8,6,64]{2,1,0:T(8,128)S(1)} all-gather(f32[1,6,64]{2,1,0:T(8,128)S(1)} %convolution_bitcast_fusion.6), channel_id=1, replica_groups=mesh['sub'=4,'wide'=8] {'wide'}, dimensions={0}, use_global_device_ids=true | all-gather | bytes 13824 | tf_op jit(solution)/shard_map/all_gather | solution.py:65
  69.8 4.3 %collective-permute-start.7 = (f32[1,1,64,128]{3,2,1,0:T(8,128)S(1)}, f32[1,1,64,128]{3,2,1,0:T(8,128)S(1)}, u32[]{:S(2)}, u32[]{:S(2)}) collective-permute-start(f32[1,1,64,128]{3,2,1,0:T(8,128)S(1)} %get-tuple-element.41), channel_id=1, source_target_pairs={{1,0},{2,1},{3,2},{4,3},{5,4},{6,5},{7,6},{9,8},{10,9},{11,10},{12... | collective-permute-start | bytes 98312 | tf_op jit(solution)/shard_map/ppermute | solution.py:27
  77.2 4.2 %collective-permute-done.5 = f32[1,64,128]{2,1,0:T(8,128)S(1)} collective-permute-done((f32[1,64,128]{2,1,0:T(8,128)S(1)}, f32[1,64,128]{2,1,0:T(8,128)S(1)}, u32[]{:S(2)}, u32[]{:S(2)}) %collective-permute-start.5) | collective-permute-done | bytes 32800 | tf_op jit(solution)/shard_map/ppermute | solution.py:27
  84.3 4.5 %collective-permute-start.11 = (f32[1,1,64,128]{3,2,1,0:T(8,128)S(1)}, f32[1,1,64,128]{3,2,1,0:T(8,128)S(1)}, u32[]{:S(2)}, u32[]{:S(2)}) collective-permute-start(f32[1,1,64,128]{3,2,1,0:T(8,128)S(1)} %get-tuple-element.33), channel_id=1, source_target_pairs={{1,0},{2,1},{3,2},{4,3},{5,4},{6,5},{7,6},{9,8},{10,9},{11,10},{12... | collective-permute-start | bytes 98312 | tf_op jit(solution)/shard_map/ppermute | solution.py:27
  88.8 3.8 %collective-permute-start.8 = (f32[1,64,128]{2,1,0:T(8,128)S(1)}, f32[1,64,128]{2,1,0:T(8,128)S(1)}, u32[]{:S(2)}, u32[]{:S(2)}) collective-permute-start(f32[1,64,128]{2,1,0:T(8,128)S(1)} %get-tuple-element.31), channel_id=1, source_target_pairs={{0,8},{8,16},{16,24},{1,9},{9,17},{17,25},{2,10},{10,18},{18,26},{... | collective-permute-start | bytes 98312 | tf_op jit(solution)/shard_map/ppermute | solution.py:25
  94.2 4.2 %collective-permute-done.9 = f32[1,64,128]{2,1,0:T(8,128)S(1)} collective-permute-done((f32[1,64,128]{2,1,0:T(8,128)S(1)}, f32[1,64,128]{2,1,0:T(8,128)S(1)}, u32[]{:S(2)}, u32[]{:S(2)}) %collective-permute-start.9) | collective-permute-done | bytes 32800 | tf_op jit(solution)/shard_map/ppermute | solution.py:27
  99.4 16.0 %psum.44 = f32[64,48]{0,1:T(8,128)S(1)} all-reduce(f32[64,48]{0,1:T(8,128)S(1)} %fusion.43), channel_id=1, replica_groups=mesh['sub'=4,'wide'=8] {'sub'}, use_global_device_ids=true, to_apply=%region_2.3 | all-reduce | flops 3072 | bytes 24576 | tf_op jit(solution)/shard_map/psum | solution.py:13
  115.4 22.4 %psum.45 = f32[64,48]{0,1:T(8,128)S(1)} all-reduce(f32[64,48]{0,1:T(8,128)S(1)} %psum.44), channel_id=1, replica_groups=mesh['sub'=4,'wide'=8] {'wide'}, use_global_device_ids=true, to_apply=%region_3.4 | all-reduce | flops 3072 | bytes 24576 | tf_op jit(solution)/shard_map/psum | solution.py:13
  137.9 7.2 %all-gather.1 = f32[8,6,64]{2,1,0:T(8,128)S(1)} all-gather(f32[1,6,64]{2,1,0:T(8,128)S(1)} %convolution_bitcast_fusion.5), channel_id=1, replica_groups=mesh['sub'=4,'wide'=8] {'wide'}, dimensions={0}, use_global_device_ids=true | all-gather | bytes 13824 | tf_op jit(solution)/shard_map/all_gather | solution.py:65
  148.4 4.2 %collective-permute-start.15 = (f32[1,1,64,128]{3,2,1,0:T(8,128)S(1)}, f32[1,1,64,128]{3,2,1,0:T(8,128)S(1)}, u32[]{:S(2)}, u32[]{:S(2)}) collective-permute-start(f32[1,1,64,128]{3,2,1,0:T(8,128)S(1)} %get-tuple-element.25), channel_id=1, source_target_pairs={{1,0},{2,1},{3,2},{4,3},{5,4},{6,5},{7,6},{9,8},{10,9},{11,10},{12... | collective-permute-start | bytes 98312 | tf_op jit(solution)/shard_map/ppermute | solution.py:27
  156.1 4.2 %collective-permute-done.13 = f32[1,64,128]{2,1,0:T(8,128)S(1)} collective-permute-done((f32[1,64,128]{2,1,0:T(8,128)S(1)}, f32[1,64,128]{2,1,0:T(8,128)S(1)}, u32[]{:S(2)}, u32[]{:S(2)}) %collective-permute-start.13) | collective-permute-done | bytes 32800 | tf_op jit(solution)/shard_map/ppermute | solution.py:27
  163.2 4.5 %collective-permute-start.19 = (f32[1,1,64,128]{3,2,1,0:T(8,128)S(1)}, f32[1,1,64,128]{3,2,1,0:T(8,128)S(1)}, u32[]{:S(2)}, u32[]{:S(2)}) collective-permute-start(f32[1,1,64,128]{3,2,1,0:T(8,128)S(1)} %get-tuple-element.17), channel_id=1, source_target_pairs={{1,0},{2,1},{3,2},{4,3},{5,4},{6,5},{7,6},{9,8},{10,9},{11,10},{12... | collective-permute-start | bytes 98312 | tf_op jit(solution)/shard_map/ppermute | solution.py:27
  167.8 3.1 %collective-permute-start.16 = (f32[1,64,128]{2,1,0:T(8,128)S(1)}, f32[1,64,128]{2,1,0:T(8,128)S(1)}, u32[]{:S(2)}, u32[]{:S(2)}) collective-permute-start(f32[1,64,128]{2,1,0:T(8,128)S(1)} %get-tuple-element.15), channel_id=1, source_target_pairs={{0,8},{8,16},{16,24},{1,9},{9,17},{17,25},{2,10},{10,18},{18,26},{... | collective-permute-start | bytes 98312 | tf_op jit(solution)/shard_map/ppermute | solution.py:25
  172.5 4.2 %collective-permute-done.17 = f32[1,64,128]{2,1,0:T(8,128)S(1)} collective-permute-done((f32[1,64,128]{2,1,0:T(8,128)S(1)}, f32[1,64,128]{2,1,0:T(8,128)S(1)}, u32[]{:S(2)}, u32[]{:S(2)}) %collective-permute-start.17) | collective-permute-done | bytes 32800 | tf_op jit(solution)/shard_map/ppermute | solution.py:27
  178.2 17.4 %psum.46 = f32[64,48]{0,1:T(8,128)S(1)} all-reduce(f32[64,48]{0,1:T(8,128)S(1)} %fusion.42), channel_id=1, replica_groups=mesh['sub'=4,'wide'=8] {'sub'}, use_global_device_ids=true, to_apply=%region_4.5 | all-reduce | flops 3072 | bytes 24576 | tf_op jit(solution)/shard_map/psum | solution.py:13
  195.6 22.4 %psum.47 = f32[64,48]{0,1:T(8,128)S(1)} all-reduce(f32[64,48]{0,1:T(8,128)S(1)} %psum.46), channel_id=1, replica_groups=mesh['sub'=4,'wide'=8] {'wide'}, use_global_device_ids=true, to_apply=%region_5.6 | all-reduce | flops 3072 | bytes 24576 | tf_op jit(solution)/shard_map/psum | solution.py:13
  218.1 7.0 %all-gather.2 = f32[8,6,64]{2,1,0:T(8,128)S(1)} all-gather(f32[1,6,64]{2,1,0:T(8,128)S(1)} %convolution_bitcast_fusion.4), channel_id=1, replica_groups=mesh['sub'=4,'wide'=8] {'wide'}, dimensions={0}, use_global_device_ids=true | all-gather | bytes 13824 | tf_op jit(solution)/shard_map/all_gather | solution.py:65
  227.7 4.4 %collective-permute-start.23 = (f32[1,1,64,128]{3,2,1,0:T(8,128)S(1)}, f32[1,1,64,128]{3,2,1,0:T(8,128)S(1)}, u32[]{:S(2)}, u32[]{:S(2)}) collective-permute-start(f32[1,1,64,128]{3,2,1,0:T(8,128)S(1)} %get-tuple-element.9), channel_id=1, source_target_pairs={{1,0},{2,1},{3,2},{4,3},{5,4},{6,5},{7,6},{9,8},{10,9},{11,10},{12... | collective-permute-start | bytes 98312 | tf_op jit(solution)/shard_map/ppermute | solution.py:27
  235.0 4.2 %collective-permute-done.21 = f32[1,64,128]{2,1,0:T(8,128)S(1)} collective-permute-done((f32[1,64,128]{2,1,0:T(8,128)S(1)}, f32[1,64,128]{2,1,0:T(8,128)S(1)}, u32[]{:S(2)}, u32[]{:S(2)}) %collective-permute-start.21) | collective-permute-done | bytes 32800 | tf_op jit(solution)/shard_map/ppermute | solution.py:27
  (115 shorter events, 39.0 us)
Async XLA Ops:
  0.9 12.7 %collective-permute-start = (f32[1,64,128]{2,1,0:T(8,128)S(1)}, f32[1,64,128]{2,1,0:T(8,128)S(1)}, u32[]{:S(2)}, u32[]{:S(2)}) collective-permute-start(f32[1,64,128]{2,1,0:T(8,128)S(1)} %get-tuple-element.47), channel_id=1, source_target_pairs={{0,8},{8,16},{16,24},{1,9},{9,17},{17,25},{2,10},{10,18},{18,26},{... | collective-permute-start | bytes 98312 | tf_op jit(solution)/shard_map/ppermute | solution.py:25
  4.4 9.1 %collective-permute-start.2 = (f32[1,1,64,128]{3,2,1,0:T(8,128)S(1)}, f32[1,1,64,128]{3,2,1,0:T(8,128)S(1)}, u32[]{:S(2)}, u32[]{:S(2)}) collective-permute-start(f32[1,1,64,128]{3,2,1,0:T(8,128)S(1)} %get-tuple-element.48), channel_id=1, source_target_pairs={{0,1},{1,2},{2,3},{3,4},{4,5},{5,6},{6,7},{8,9},{9,10},{10,11},{11... | collective-permute-start | bytes 98312 | tf_op jit(solution)/shard_map/ppermute | solution.py:25
  6.4 7.2 %collective-permute-start.3 = (f32[1,1,64,128]{3,2,1,0:T(8,128)S(1)}, f32[1,1,64,128]{3,2,1,0:T(8,128)S(1)}, u32[]{:S(2)}, u32[]{:S(2)}) collective-permute-start(f32[1,1,64,128]{3,2,1,0:T(8,128)S(1)} %get-tuple-element.49), channel_id=1, source_target_pairs={{1,0},{2,1},{3,2},{4,3},{5,4},{6,5},{7,6},{9,8},{10,9},{11,10},{12... | collective-permute-start | bytes 98312 | tf_op jit(solution)/shard_map/ppermute | solution.py:27
  10.9 5.8 %collective-permute-start.1 = (f32[1,64,128]{2,1,0:T(8,128)S(1)}, f32[1,64,128]{2,1,0:T(8,128)S(1)}, u32[]{:S(2)}, u32[]{:S(2)}) collective-permute-start(f32[1,64,128]{2,1,0:T(8,128)S(1)} %get-tuple-element.50), channel_id=1, source_target_pairs={{8,0},{16,8},{24,16},{9,1},{17,9},{25,17},{10,2},{18,10},{26,18},{... | collective-permute-start | bytes 98312 | tf_op jit(solution)/shard_map/ppermute | solution.py:27
  67.6 9.3 %collective-permute-start.6 = (f32[1,1,64,128]{3,2,1,0:T(8,128)S(1)}, f32[1,1,64,128]{3,2,1,0:T(8,128)S(1)}, u32[]{:S(2)}, u32[]{:S(2)}) collective-permute-start(f32[1,1,64,128]{3,2,1,0:T(8,128)S(1)} %get-tuple-element.40), channel_id=1, source_target_pairs={{0,1},{1,2},{2,3},{3,4},{4,5},{5,6},{6,7},{8,9},{9,10},{10,11},{11... | collective-permute-start | bytes 98312 | tf_op jit(solution)/shard_map/ppermute | solution.py:25
  69.8 7.1 %collective-permute-start.7 = (f32[1,1,64,128]{3,2,1,0:T(8,128)S(1)}, f32[1,1,64,128]{3,2,1,0:T(8,128)S(1)}, u32[]{:S(2)}, u32[]{:S(2)}) collective-permute-start(f32[1,1,64,128]{3,2,1,0:T(8,128)S(1)} %get-tuple-element.41), channel_id=1, source_target_pairs={{1,0},{2,1},{3,2},{4,3},{5,4},{6,5},{7,6},{9,8},{10,9},{11,10},{12... | collective-permute-start | bytes 98312 | tf_op jit(solution)/shard_map/ppermute | solution.py:27
  74.3 2.9 %collective-permute-start.4 = (f32[1,64,128]{2,1,0:T(8,128)S(1)}, f32[1,64,128]{2,1,0:T(8,128)S(1)}, u32[]{:S(2)}, u32[]{:S(2)}) collective-permute-start(f32[1,64,128]{2,1,0:T(8,128)S(1)} %get-tuple-element.39), channel_id=1, source_target_pairs={{0,8},{8,16},{16,24},{1,9},{9,17},{17,25},{2,10},{10,18},{18,26},{... | collective-permute-start | bytes 98312 | tf_op jit(solution)/shard_map/ppermute | solution.py:25
  75.6 5.8 %collective-permute-start.5 = (f32[1,64,128]{2,1,0:T(8,128)S(1)}, f32[1,64,128]{2,1,0:T(8,128)S(1)}, u32[]{:S(2)}, u32[]{:S(2)}) collective-permute-start(f32[1,64,128]{2,1,0:T(8,128)S(1)} %get-tuple-element.42), channel_id=1, source_target_pairs={{8,0},{16,8},{24,16},{9,1},{17,9},{25,17},{10,2},{18,10},{26,18},{... | collective-permute-start | bytes 98312 | tf_op jit(solution)/shard_map/ppermute | solution.py:27
  82.4 11.6 %collective-permute-start.10 = (f32[1,1,64,128]{3,2,1,0:T(8,128)S(1)}, f32[1,1,64,128]{3,2,1,0:T(8,128)S(1)}, u32[]{:S(2)}, u32[]{:S(2)}) collective-permute-start(f32[1,1,64,128]{3,2,1,0:T(8,128)S(1)} %get-tuple-element.32), channel_id=1, source_target_pairs={{0,1},{1,2},{2,3},{3,4},{4,5},{5,6},{6,7},{8,9},{9,10},{10,11},{11... | collective-permute-start | bytes 98312 | tf_op jit(solution)/shard_map/ppermute | solution.py:25
  84.3 9.7 %collective-permute-start.11 = (f32[1,1,64,128]{3,2,1,0:T(8,128)S(1)}, f32[1,1,64,128]{3,2,1,0:T(8,128)S(1)}, u32[]{:S(2)}, u32[]{:S(2)}) collective-permute-start(f32[1,1,64,128]{3,2,1,0:T(8,128)S(1)} %get-tuple-element.33), channel_id=1, source_target_pairs={{1,0},{2,1},{3,2},{4,3},{5,4},{6,5},{7,6},{9,8},{10,9},{11,10},{12... | collective-permute-start | bytes 98312 | tf_op jit(solution)/shard_map/ppermute | solution.py:27
  88.8 5.4 %collective-permute-start.8 = (f32[1,64,128]{2,1,0:T(8,128)S(1)}, f32[1,64,128]{2,1,0:T(8,128)S(1)}, u32[]{:S(2)}, u32[]{:S(2)}) collective-permute-start(f32[1,64,128]{2,1,0:T(8,128)S(1)} %get-tuple-element.31), channel_id=1, source_target_pairs={{0,8},{8,16},{16,24},{1,9},{9,17},{17,25},{2,10},{10,18},{18,26},{... | collective-permute-start | bytes 98312 | tf_op jit(solution)/shard_map/ppermute | solution.py:25
  92.6 5.8 %collective-permute-start.9 = (f32[1,64,128]{2,1,0:T(8,128)S(1)}, f32[1,64,128]{2,1,0:T(8,128)S(1)}, u32[]{:S(2)}, u32[]{:S(2)}) collective-permute-start(f32[1,64,128]{2,1,0:T(8,128)S(1)} %get-tuple-element.34), channel_id=1, source_target_pairs={{8,0},{16,8},{24,16},{9,1},{17,9},{25,17},{10,2},{18,10},{26,18},{... | collective-permute-start | bytes 98312 | tf_op jit(solution)/shard_map/ppermute | solution.py:27
  146.2 9.6 %collective-permute-start.14 = (f32[1,1,64,128]{3,2,1,0:T(8,128)S(1)}, f32[1,1,64,128]{3,2,1,0:T(8,128)S(1)}, u32[]{:S(2)}, u32[]{:S(2)}) collective-permute-start(f32[1,1,64,128]{3,2,1,0:T(8,128)S(1)} %get-tuple-element.24), channel_id=1, source_target_pairs={{0,1},{1,2},{2,3},{3,4},{4,5},{5,6},{6,7},{8,9},{9,10},{10,11},{11... | collective-permute-start | bytes 98312 | tf_op jit(solution)/shard_map/ppermute | solution.py:25
  148.4 7.4 %collective-permute-start.15 = (f32[1,1,64,128]{3,2,1,0:T(8,128)S(1)}, f32[1,1,64,128]{3,2,1,0:T(8,128)S(1)}, u32[]{:S(2)}, u32[]{:S(2)}) collective-permute-start(f32[1,1,64,128]{3,2,1,0:T(8,128)S(1)} %get-tuple-element.25), channel_id=1, source_target_pairs={{1,0},{2,1},{3,2},{4,3},{5,4},{6,5},{7,6},{9,8},{10,9},{11,10},{12... | collective-permute-start | bytes 98312 | tf_op jit(solution)/shard_map/ppermute | solution.py:27
  152.7 3.4 %collective-permute-start.12 = (f32[1,64,128]{2,1,0:T(8,128)S(1)}, f32[1,64,128]{2,1,0:T(8,128)S(1)}, u32[]{:S(2)}, u32[]{:S(2)}) collective-permute-start(f32[1,64,128]{2,1,0:T(8,128)S(1)} %get-tuple-element.23), channel_id=1, source_target_pairs={{0,8},{8,16},{16,24},{1,9},{9,17},{17,25},{2,10},{10,18},{18,26},{... | collective-permute-start | bytes 98312 | tf_op jit(solution)/shard_map/ppermute | solution.py:25
  154.5 5.8 %collective-permute-start.13 = (f32[1,64,128]{2,1,0:T(8,128)S(1)}, f32[1,64,128]{2,1,0:T(8,128)S(1)}, u32[]{:S(2)}, u32[]{:S(2)}) collective-permute-start(f32[1,64,128]{2,1,0:T(8,128)S(1)} %get-tuple-element.26), channel_id=1, source_target_pairs={{8,0},{16,8},{24,16},{9,1},{17,9},{25,17},{10,2},{18,10},{26,18},{... | collective-permute-start | bytes 98312 | tf_op jit(solution)/shard_map/ppermute | solution.py:27
  161.3 10.9 %collective-permute-start.18 = (f32[1,1,64,128]{3,2,1,0:T(8,128)S(1)}, f32[1,1,64,128]{3,2,1,0:T(8,128)S(1)}, u32[]{:S(2)}, u32[]{:S(2)}) collective-permute-start(f32[1,1,64,128]{3,2,1,0:T(8,128)S(1)} %get-tuple-element.16), channel_id=1, source_target_pairs={{0,1},{1,2},{2,3},{3,4},{4,5},{5,6},{6,7},{8,9},{9,10},{10,11},{11... | collective-permute-start | bytes 98312 | tf_op jit(solution)/shard_map/ppermute | solution.py:25
  163.2 9.0 %collective-permute-start.19 = (f32[1,1,64,128]{3,2,1,0:T(8,128)S(1)}, f32[1,1,64,128]{3,2,1,0:T(8,128)S(1)}, u32[]{:S(2)}, u32[]{:S(2)}) collective-permute-start(f32[1,1,64,128]{3,2,1,0:T(8,128)S(1)} %get-tuple-element.17), channel_id=1, source_target_pairs={{1,0},{2,1},{3,2},{4,3},{5,4},{6,5},{7,6},{9,8},{10,9},{11,10},{12... | collective-permute-start | bytes 98312 | tf_op jit(solution)/shard_map/ppermute | solution.py:27
  167.8 4.7 %collective-permute-start.16 = (f32[1,64,128]{2,1,0:T(8,128)S(1)}, f32[1,64,128]{2,1,0:T(8,128)S(1)}, u32[]{:S(2)}, u32[]{:S(2)}) collective-permute-start(f32[1,64,128]{2,1,0:T(8,128)S(1)} %get-tuple-element.15), channel_id=1, source_target_pairs={{0,8},{8,16},{16,24},{1,9},{9,17},{17,25},{2,10},{10,18},{18,26},{... | collective-permute-start | bytes 98312 | tf_op jit(solution)/shard_map/ppermute | solution.py:25
  170.9 5.8 %collective-permute-start.17 = (f32[1,64,128]{2,1,0:T(8,128)S(1)}, f32[1,64,128]{2,1,0:T(8,128)S(1)}, u32[]{:S(2)}, u32[]{:S(2)}) collective-permute-start(f32[1,64,128]{2,1,0:T(8,128)S(1)} %get-tuple-element.18), channel_id=1, source_target_pairs={{8,0},{16,8},{24,16},{9,1},{17,9},{25,17},{10,2},{18,10},{26,18},{... | collective-permute-start | bytes 98312 | tf_op jit(solution)/shard_map/ppermute | solution.py:27
  225.6 9.1 %collective-permute-start.22 = (f32[1,1,64,128]{3,2,1,0:T(8,128)S(1)}, f32[1,1,64,128]{3,2,1,0:T(8,128)S(1)}, u32[]{:S(2)}, u32[]{:S(2)}) collective-permute-start(f32[1,1,64,128]{3,2,1,0:T(8,128)S(1)} %get-tuple-element.8), channel_id=1, source_target_pairs={{0,1},{1,2},{2,3},{3,4},{4,5},{5,6},{6,7},{8,9},{9,10},{10,11},{11... | collective-permute-start | bytes 98312 | tf_op jit(solution)/shard_map/ppermute | solution.py:25
  227.7 7.0 %collective-permute-start.23 = (f32[1,1,64,128]{3,2,1,0:T(8,128)S(1)}, f32[1,1,64,128]{3,2,1,0:T(8,128)S(1)}, u32[]{:S(2)}, u32[]{:S(2)}) collective-permute-start(f32[1,1,64,128]{3,2,1,0:T(8,128)S(1)} %get-tuple-element.9), channel_id=1, source_target_pairs={{1,0},{2,1},{3,2},{4,3},{5,4},{6,5},{7,6},{9,8},{10,9},{11,10},{12... | collective-permute-start | bytes 98312 | tf_op jit(solution)/shard_map/ppermute | solution.py:27
  232.1 2.9 %collective-permute-start.20 = (f32[1,64,128]{2,1,0:T(8,128)S(1)}, f32[1,64,128]{2,1,0:T(8,128)S(1)}, u32[]{:S(2)}, u32[]{:S(2)}) collective-permute-start(f32[1,64,128]{2,1,0:T(8,128)S(1)} %get-tuple-element.7), channel_id=1, source_target_pairs={{0,8},{8,16},{16,24},{1,9},{9,17},{17,25},{2,10},{10,18},{18,26},{... | collective-permute-start | bytes 98312 | tf_op jit(solution)/shard_map/ppermute | solution.py:25
  233.4 5.8 %collective-permute-start.21 = (f32[1,64,128]{2,1,0:T(8,128)S(1)}, f32[1,64,128]{2,1,0:T(8,128)S(1)}, u32[]{:S(2)}, u32[]{:S(2)}) collective-permute-start(f32[1,64,128]{2,1,0:T(8,128)S(1)} %get-tuple-element.10), channel_id=1, source_target_pairs={{8,0},{16,8},{24,16},{9,1},{17,9},{25,17},{10,2},{18,10},{26,18},{... | collective-permute-start | bytes 98312 | tf_op jit(solution)/shard_map/ppermute | solution.py:27
  (7 other events, 33.0 us)
